TPU v7x, 32 devices: a whole 2x2x4 slice. The times are simulated.
32 devices in a mesh: groups: 2 (over y), tm: 4 (over x, core), win: 4 (over z).
Axes of the slice: x: 2, y: 2, z: 4, core: 2. Of those that a mesh axis runs over, the one named last changes fastest.
Arguments:
- unitaries: float32 [8, 4, 2, 2, 256, 256], P(('groups', 'win'), 'tm'), parts along dimension 0, may hold values from -1 to 1, as said below
Outputs:
- propagators: float32 [8, 4, 2, 2, 256, 256], P(('groups', 'win'), 'tm'), parts along dimension 0
There are 2 independent parts, one for each index of `groups`. A program takes and returns all parts, laid end to end along the dimension named above; each array names one. Nothing has to cross between parts.
Inputs may be any that keep to these rules, and one draw needn't show every extreme that they name: `unitaries`: each slot's complex matrix is unitary.
All inputs are finite; a program needn't handle non-finite values.
Results may differ from a plain program's by a relative error of at most 0.0003.
Values sent between devices are 32-bit elements; how exact they have to be, the bound alone decides.
A program may use at most 64 MiB of HBM per device.

v0:
```python
import jax
import jax.numpy as jnp
from jax import lax
from jax.sharding import PartitionSpec as P


def prefix(value, axis, join, neutral):
    count, mine = (lax.axis_size(axis), lax.axis_index(axis))
    pieces = lax.all_gather(value, axis)
    running = jnp.full_like(value, 0) + jnp.asarray(neutral, value.dtype)

    def hop(position, running):
        longer = join(running, pieces[position])
        return jnp.where(position < mine, longer, running)

    return lax.fori_loop(0, count - 1, hop, running)


def from_root(value, axis, source):
    kept = jnp.where(lax.axis_index(axis) == source, value, 0).astype(value.dtype)
    return lax.psum(kept, axis)


def complex_product(left, right):
    hi = lax.Precision.HIGHEST
    real_part = jnp.dot(
        left[0], right[0], precision=hi, preferred_element_type=jnp.float32
    ) - jnp.dot(left[1], right[1], precision=hi, preferred_element_type=jnp.float32)
    imag_part = jnp.dot(
        left[0], right[1], precision=hi, preferred_element_type=jnp.float32
    ) + jnp.dot(left[1], right[0], precision=hi, preferred_element_type=jnp.float32)
    return jnp.stack([real_part, imag_part])


def later_first(earlier, later):
    return complex_product(later, earlier)


def on_device(unitaries):
    own_slots = unitaries[0, 0]
    width = own_slots.shape[-1]
    identity_pair = jnp.stack(
        [jnp.eye(width, dtype=jnp.float32), jnp.zeros((width, width), jnp.float32)]
    )
    prefixes = [own_slots[0]]
    prefixes.append(complex_product(own_slots[1], prefixes[-1]))
    block_total = prefixes[-1]
    before = prefix(block_total, "tm", later_first, identity_pair)
    through = complex_product(block_total, before)
    window_product = from_root(through, "tm", lax.axis_size("tm") - 1)
    window_carry = prefix(window_product, "win", later_first, identity_pair)
    offset = complex_product(before, window_carry)
    results = jnp.stack([complex_product(piece, offset) for piece in prefixes])
    return results[None, None]


def solution(mesh):
    placed = (P(("groups", "win"), "tm", None, None, None, None),)
    return jax.shard_map(
        on_device,
        mesh=mesh,
        in_specs=placed,
        out_specs=P(("groups", "win"), "tm", None, None, None, None),
        check_vma=False,
    )
```

profile of v0, /device:TPU:0, one launch (start us, length us, event | category | flops | bytes accessed | tf_op | source)
XLA Modules:
  0.0 168.4 jit_solution(17108181392384072371)
XLA Ops:
  6.5 1.5 fusion.67
  8.0 1.4 fusion.57
  9.5 1.4 convolution_subtract_fusion.6
  10.9 0.4 convolution_add_fusion.6
  11.3 0.8 pad_maximum_fusion
  12.3 25.3 %all-gather.6.cloned.1.call-done = f32[8,256,256]{2,1,0:T(8,128)} async-done(((f32[2,256,256]{2,1,0:T(8,128)}), f32[8,256,256]{2,1,0:T(8,128)}) %all-gather.6.cloned.1.call-update) | async-done | bytes 2097168 | tf_op jit(solution)/shard_map/all_gather | solution.py:9
  37.6 16.6 %while.26 = (s32[]{:T(128)}, f32[2,256,256]{2,1,0:T(8,128)S(1)}, s32[]{:T(128)}, f32[4,2,256,256]{3,2,1,0:T(8,128)}, s32[]{:T(128)}, /*index=5*/s32[]{:T(128)}, s32[]{}) while((s32[]{:T(128)}, f32[2,256,256]{2,1,0:T(8,128)S(1)}, s32[]{:T(128)}, f32[4,2,256,256]{3,2,1,0:T(8,128)}, s32[]{:T(128)}, /*index=5*/s32[]{:T(128)}, s32[]{}) %tuple.64), condition=%wide.region_1.2_spmd, body=%wide.region_0.1_spmd.sunk | while | flops 805699584 | bytes 5245035 | solution.py:16
  37.6 1.3 fusion.133
  38.9 1.3 fusion.134
  40.2 1.3 fusion.135
  41.6 1.3 fusion.136
  43.1 1.3 fusion.133
  44.4 1.3 fusion.134
  45.8 1.3 fusion.135
  47.1 1.3 fusion.136
  48.6 1.3 fusion.133
  49.9 1.3 fusion.134
  51.3 1.3 fusion.135
  52.6 1.3 fusion.136
  54.1 0.4 fusion.53
  54.5 0.4 fusion.47
  55.7 0.8 fusion.38
  56.8 33.1 %all-reduce.3.cloned.1.call-done = f32[1,2,256,256]{3,2,1,0:T(8,128)} async-done(((f32[1,2,256,256]{3,2,1,0:T(8,128)}), f32[1,2,256,256]{3,2,1,0:T(8,128)}) %all-reduce.3.cloned.1.call-update) | async-done | bytes 524304 | tf_op jit(solution)/shard_map/psum | solution.py:21
  89.9 47.5 %all-gather.4.cloned.1.call-done = f32[4,2,256,256]{3,2,1,0:T(8,128)} async-done(((f32[1,2,256,256]{3,2,1,0:T(8,128)}), f32[4,2,256,256]{3,2,1,0:T(8,128)}) %all-gather.4.cloned.1.call-update) | async-done | bytes 2097168 | tf_op jit(solution)/shard_map/all_gather | solution.py:9
  137.4 16.6 %while.27 = (s32[]{:T(128)}, f32[2,256,256]{2,1,0:T(8,128)S(1)}, s32[]{:T(128)}, f32[4,2,256,256]{3,2,1,0:T(8,128)}, s32[]{:T(128)}, /*index=5*/s32[]{:T(128)}, s32[]{}) while((s32[]{:T(128)}, f32[2,256,256]{2,1,0:T(8,128)S(1)}, s32[]{:T(128)}, f32[4,2,256,256]{3,2,1,0:T(8,128)}, s32[]{:T(128)}, /*index=5*/s32[]{:T(128)}, s32[]{}) %tuple.55), condition=%wide.region_4.5_spmd, body=%wide.region_3.4_spmd.sunk | while | flops 805699584 | bytes 5245035 | solution.py:16
  137.4 1.3 fusion.141
  138.8 1.3 fusion.142
  140.1 1.3 fusion.143
  141.4 1.3 fusion.144
  142.9 1.3 fusion.141
  144.3 1.3 fusion.142
  145.6 1.3 fusion.143
  147.0 1.3 fusion.144
  148.5 1.3 fusion.141
  149.8 1.3 fusion.142
  151.1 1.3 fusion.143
  152.5 1.3 fusion.144
  154.8 0.4 convolution_subtract_fusion.4
  155.2 0.6 fusion.95
  155.8 0.6 fusion.64
  156.4 0.4 convolution_add_fusion.4
  156.7 0.6 fusion.96
  157.4 0.6 fusion.62
  158.0 0.6 fusion.33
  158.6 0.6 fusion.32
  159.2 0.6 fusion.35
  159.8 0.6 fusion.34
  160.6 1.3 copy.11
  (23 shorter events, 2.9 us)
Async XLA Ops:
  6.5 4.3 %copy-start = (f32[1,1,2,2,256,256]{5,4,3,2,1,0:T(8,128)S(1)}, f32[1,1,2,2,256,256]{5,4,3,2,1,0:T(8,128)}, u32[]{:S(2)}) copy-start(f32[1,1,2,2,256,256]{5,4,3,2,1,0:T(8,128)} %param.5) | copy-start | bytes 3145732
  6.5 31.0 %all-gather.6.cloned.1.call-start = ((), (), s32[]{:S(2)}) async-start(), calls=%async_computation.2 | async-start | bytes 2621440 | tf_op jit(solution)/shard_map/all_gather | solution.py:9
  12.1 77.7 %all-reduce.3.cloned.1.call-start = ((), (), s32[]{:S(2)}) async-start(), calls=%async_computation | async-start | bytes 1048576 | tf_op jit(solution)/shard_map/psum | solution.py:21
  56.5 80.9 %all-gather.4.cloned.1.call-start = ((), (), s32[]{:S(2)}) async-start(), calls=%async_computation.1 | async-start | bytes 2621440 | tf_op jit(solution)/shard_map/all_gather | solution.py:9
Sparse Core Ops, SparseCore 0:
  12.3 25.2 all-gather.5
  56.7 33.1 all-reduce.2
  91.4 45.9 all-gather.3
where the time goes:
time: 169 us; the launch traced here: 168 us
  waiting for transfers between devices  106 us (63%)
  matrix products  44.5 us (26%)
  between operations  13.3 us (8%)
  other arithmetic  2.66 us (2%)
    all_gather x2, waiting for transfers between devices, prefix(): pieces = lax.all_gather(value, axis)  72.8 us
    psum x1, waiting for transfers between devices, from_root(): return lax.psum(kept, axis)  33.1 us
    dot_general x11, matrix products, complex_product(): jnp.dot(left[0], right[0], precision=hi, preferred_element_type=jnp.float32)  11.5 us
    dot_general x11, matrix products, complex_product(): jnp.dot(left[1], right[1], precision=hi, preferred_element_type=jnp.float32)  11.4 us
    dot_general x11, matrix products, complex_product(): jnp.dot(left[0], right[1], precision=hi, preferred_element_type=jnp.float32)  11.3 us
    dot_general x11, matrix products, complex_product(): jnp.dot(left[1], right[0], precision=hi, preferred_element_type=jnp.float32)  10.4 us
  transfers between devices with their start and end apart: 3, of which 3 were waited for; matrix products, arithmetic and copies ran while one was open for 0% of the time, Pallas kernels for 0%

commit v1 on v0

--- a/solution.py
+++ b/solution.py
@@ -18,7 +18,7 @@
 
 def from_root(value, axis, source):
     kept = jnp.where(lax.axis_index(axis) == source, value, 0).astype(value.dtype)
-    return lax.psum(kept, axis)
+    return jnp.sum(lax.all_gather(kept, axis), axis=0)
 
 
 def complex_product(left, right):

time: 169 us -> 160 us (0.947)
  waiting for transfers between devices: 106 us -> 93.9 us
  other arithmetic: 2.66 us -> 5.24 us
    psum x1 -> x0, waiting for transfers between devices: 33.1 us -> none  [from_root(): return lax.psum(kept, axis)]
    all_gather x0 -> x1, waiting for transfers between devices: none -> 22.5 us  [from_root(): return jnp.sum(lax.all_gather(kept, axis), axis=0)]
    reduce_sum x0 -> x1, other arithmetic: none -> 2.58 us  [from_root(): return jnp.sum(lax.all_gather(kept, axis), axis=0)]
where the time goes in v1:
time: 160 us; the launch traced here: 159 us
  waiting for transfers between devices  93.9 us (59%)
  matrix products  44.5 us (28%)
  between operations  13.3 us (8%)
  other arithmetic  5.24 us (3%)
    all_gather x2, waiting for transfers between devices, prefix(): pieces = lax.all_gather(value, axis)  71.4 us
    all_gather x1, waiting for transfers between devices, from_root(): return jnp.sum(lax.all_gather(kept, axis), axis=0)  22.5 us
    dot_general x11, matrix products, complex_product(): jnp.dot(left[0], right[0], precision=hi, preferred_element_type=jnp.float32)  11.4 us
    dot_general x11, matrix products, complex_product(): jnp.dot(left[1], right[1], precision=hi, preferred_element_type=jnp.float32)  11.4 us
    dot_general x11, matrix products, complex_product(): jnp.dot(left[0], right[1], precision=hi, preferred_element_type=jnp.float32)  11.3 us
    dot_general x11, matrix products, complex_product(): jnp.dot(left[1], right[0], precision=hi, preferred_element_type=jnp.float32)  10.4 us
  transfers between devices with their start and end apart: 3, of which 3 were waited for; matrix products, arithmetic and copies ran while one was open for 0% of the time, Pallas kernels for 0%

profile of v1, /device:TPU:0, one launch (start us, length us, event | category | flops | bytes accessed | tf_op | source)
XLA Modules:
  0.0 159.0 jit_solution(1830578403473986447)
XLA Ops:
  6.5 1.5 fusion.66
  8.0 1.4 fusion.56
  9.5 1.4 convolution_subtract_fusion.6
  10.9 0.4 convolution_add_fusion.6
  11.3 0.8 pad_maximum_fusion
  12.3 25.3 %all-gather.8.cloned.1.call-done = f32[8,256,256]{2,1,0:T(8,128)} async-done(((f32[2,256,256]{2,1,0:T(8,128)}), f32[8,256,256]{2,1,0:T(8,128)}) %all-gather.8.cloned.1.call-update) | async-done | bytes 2097168 | tf_op jit(solution)/shard_map/all_gather | solution.py:9
  37.6 16.6 %while.26 = (s32[]{:T(128)}, f32[2,256,256]{2,1,0:T(8,128)S(1)}, s32[]{:T(128)}, f32[4,2,256,256]{3,2,1,0:T(8,128)}, s32[]{:T(128)}, /*index=5*/s32[]{:T(128)}, s32[]{}) while((s32[]{:T(128)}, f32[2,256,256]{2,1,0:T(8,128)S(1)}, s32[]{:T(128)}, f32[4,2,256,256]{3,2,1,0:T(8,128)}, s32[]{:T(128)}, /*index=5*/s32[]{:T(128)}, s32[]{}) %tuple.64), condition=%wide.region_1.2_spmd, body=%wide.region_0.1_spmd.sunk | while | flops 805699584 | bytes 5245035 | solution.py:16
  37.6 1.3 fusion.132
  38.9 1.3 fusion.133
  40.2 1.3 fusion.134
  41.6 1.3 fusion.135
  43.1 1.3 fusion.132
  44.4 1.3 fusion.133
  45.8 1.3 fusion.134
  47.1 1.3 fusion.135
  48.6 1.3 fusion.132
  50.0 1.3 fusion.133
  51.3 1.3 fusion.134
  52.6 1.3 fusion.135
  55.3 0.4 fusion.36
  55.7 0.8 maximum_select_fusion.2
  56.8 22.5 %all-gather.6.cloned.1.call-done = f32[4,2,256,256]{3,2,1,0:T(8,128)} async-done(((f32[1,2,256,256]{3,2,1,0:T(8,128)}), f32[4,2,256,256]{3,2,1,0:T(8,128)}) %all-gather.6.cloned.1.call-update) | async-done | bytes 2097168 | tf_op jit(solution)/shard_map/all_gather | solution.py:21
  79.3 2.6 %reduce_sum.9 = f32[2,256,256]{2,1,0:T(8,128)} reduce(f32[4,2,256,256]{3,2,1,0:T(8,128)} %all-gather.6.cloned.1.call-done, f32[]{:T(128)} %constant.60.clone.1), dimensions={0}, to_apply=%region_2.3 | reduce | flops 393216 | bytes 2621444 | tf_op jit(solution)/shard_map/reduce_sum | solution.py:21
  81.9 46.1 %all-gather.10.cloned.1.call-done = f32[8,256,256]{2,1,0:T(8,128)} async-done(((f32[2,256,256]{2,1,0:T(8,128)}), f32[8,256,256]{2,1,0:T(8,128)}) %all-gather.10.cloned.1.call-update) | async-done | bytes 2097168 | tf_op jit(solution)/shard_map/all_gather | solution.py:9
  128.0 16.6 %while.27 = (s32[]{:T(128)}, f32[2,256,256]{2,1,0:T(8,128)S(1)}, s32[]{:T(128)}, f32[4,2,256,256]{3,2,1,0:T(8,128)}, s32[]{:T(128)}, /*index=5*/s32[]{:T(128)}, s32[]{}) while((s32[]{:T(128)}, f32[2,256,256]{2,1,0:T(8,128)S(1)}, s32[]{:T(128)}, f32[4,2,256,256]{3,2,1,0:T(8,128)}, s32[]{:T(128)}, /*index=5*/s32[]{:T(128)}, s32[]{}) %tuple.65), condition=%wide.region_4.5_spmd, body=%wide.region_3.4_spmd.sunk | while | flops 805699584 | bytes 5245035 | solution.py:16
  128.0 1.3 fusion.140
  129.3 1.3 fusion.141
  130.7 1.3 fusion.142
  132.0 1.3 fusion.143
  133.5 1.3 fusion.140
  134.9 1.3 fusion.141
  136.2 1.3 fusion.142
  137.5 1.3 fusion.143
  139.0 1.3 fusion.140
  140.4 1.3 fusion.141
  141.7 1.3 fusion.142
  143.1 1.3 fusion.143
  145.3 0.4 convolution_subtract_fusion.4
  145.7 0.6 fusion.94
  146.3 0.6 fusion.63
  146.9 0.4 convolution_add_fusion.4
  147.3 0.6 fusion.95
  147.9 0.6 fusion.61
  148.5 0.6 fusion.33
  149.1 0.6 fusion.32
  149.7 0.6 fusion.35
  150.4 0.6 fusion.34
  151.1 1.3 copy.11
  (24 shorter events, 3.3 us)
Async XLA Ops:
  6.5 4.3 %copy-start = (f32[1,1,2,2,256,256]{5,4,3,2,1,0:T(8,128)S(1)}, f32[1,1,2,2,256,256]{5,4,3,2,1,0:T(8,128)}, u32[]{:S(2)}) copy-start(f32[1,1,2,2,256,256]{5,4,3,2,1,0:T(8,128)} %param.5) | copy-start | bytes 3145732
  6.5 31.0 %all-gather.8.cloned.1.call-start = ((), (), s32[]{:S(2)}) async-start(), calls=%async_computation.1 | async-start | bytes 2621440 | tf_op jit(solution)/shard_map/all_gather | solution.py:9
  12.1 67.2 %all-gather.6.cloned.1.call-start = ((), (), s32[]{:S(2)}) async-start(), calls=%async_computation | async-start | bytes 2621440 | tf_op jit(solution)/shard_map/all_gather | solution.py:21
  56.5 71.4 %all-gather.10.cloned.1.call-start = ((), (), s32[]{:S(2)}) async-start(), calls=%async_computation.2 | async-start | bytes 2621440 | tf_op jit(solution)/shard_map/all_gather | solution.py:9
Sparse Core Ops, SparseCore 0:
  12.3 25.2 all-gather.7
  56.7 22.5 all-gather.5
  82.0 45.9 all-gather.9
